TPU v7x, 32 devices: a whole 2x2x4 slice. The times are simulated.
32 devices in a mesh: dp: 8 (over z, x), tensor: 4 (over y, core).
Axes of the slice: x: 2, y: 2, z: 4, core: 2. Of those that a mesh axis runs over, the one named last changes fastest.
Arguments:
- tokens: bfloat16 [16384, 768], P('dp'), may hold values from -6 to 6
- seq_lens: int32 [16], P('dp'), may hold values from 512 to 1024, as said below
- block_sizes: int32 [16], P('dp'), may hold values from 128 to 512
- w_query: bfloat16 [768, 768], P('dp', 'tensor'), may hold values from -0.3125 to 0.3125
- b_query: bfloat16 [768], P('tensor'), may hold values from -3 to 3
- w_key: bfloat16 [768, 768], P('dp', 'tensor'), may hold values from -0.21875 to 0.21875
- w_value: bfloat16 [768, 768], P('dp', 'tensor'), may hold values from -0.21875 to 0.21875
- b_value: bfloat16 [768], P('tensor'), may hold values from -3 to 3
- w_out: bfloat16 [768, 768], P('tensor', 'dp'), may hold values from -1.25 to 1.25
- b_out: bfloat16 [768], P('dp'), may hold values from -2 to 2
- gain_one: bfloat16 [768], P('dp'), may hold values from 0.25 to 1.75
- shift_one: bfloat16 [768], P('dp'), may hold values from -2 to 2
- w_up: bfloat16 [768, 3072], P('dp', 'tensor'), may hold values from -0.21875 to 0.21875
- b_up: bfloat16 [3072], P('tensor'), may hold values from -3 to 3
- w_down: bfloat16 [3072, 768], P('tensor', 'dp'), may hold values from -0.109375 to 0.109375
- b_down: bfloat16 [768], P('dp'), may hold values from -2 to 2
- gain_two: bfloat16 [768], P('dp'), may hold values from 0.25 to 1.75
- shift_two: bfloat16 [768], P('dp'), may hold values from -2 to 2
- cotangent: bfloat16 [16384, 768], P('dp'), may hold values from -6 to 6
Outputs:
- output: bfloat16 [16384, 768], P('dp')
- input_grad: float32 [16384, 768], P('dp', 'tensor')
- grad_w_query: float32 [768, 768], P('dp', 'tensor')
- grad_b_query: float32 [768], P('tensor')
- grad_w_key: float32 [768, 768], P('dp', 'tensor')
- grad_w_value: float32 [768, 768], P('dp', 'tensor')
- grad_b_value: float32 [768], P('tensor')
- grad_w_out: float32 [768, 768], P('tensor', 'dp')
- grad_b_out: float32 [768], P('dp')
- grad_gain_one: float32 [768], P('dp')
- grad_shift_one: float32 [768], P('dp')
- grad_w_up: float32 [768, 3072], P('dp', 'tensor')
- grad_b_up: float32 [3072], P('tensor')
- grad_w_down: float32 [3072, 768], P('tensor', 'dp')
- grad_b_down: float32 [768], P('dp')
- grad_gain_two: float32 [768], P('dp')
- grad_shift_two: float32 [768], P('dp')
Inputs may be any that keep to these rules, and one draw needn't show every extreme that they name: seq_lens[s] counts the key positions of sequence s that any query may see; at least one sequence is whole.
All inputs are finite; a program needn't handle non-finite values.
Results may differ from a plain program's by a relative error of at most 0.015.
The roundings to bfloat16 on the way count: a program that leaves them out, or rounds other values in their place, can miss the bound.
Values may be sent and summed in bfloat16 or wider, within the bound.
A program may use at most 192 MiB of HBM per device.

v0:
```python
import jax
import jax.numpy as jnp
from jax import lax
from jax.sharding import PartitionSpec as P

HEAD = 64
norm_epsilon = 1e-12
inv_root_two = 0.7071067811865476
inv_root_tau = 0.3989422804014327
masked_score = -1000000000.0


def matmul(first_operand, second_operand):
    return jnp.dot(first_operand, second_operand, preferred_element_type=jnp.float32)


def contract_rows(first_operand, second_operand):
    return lax.dot_general(
        first_operand, second_operand, (((0,), (0,)), ((), ())), preferred_element_type=jnp.float32
    )


def contract_cols(first_operand, second_operand):
    return lax.dot_general(
        first_operand, second_operand, (((1,), (1,)), ((), ())), preferred_element_type=jnp.float32
    )


def norm_forward(row_values, gain_row, offset_row):
    row_mean = jnp.mean(row_values, axis=-1, keepdims=True)
    centred = row_values - row_mean
    variance = jnp.mean(centred * centred, axis=-1, keepdims=True)
    inv_scale = lax.rsqrt(variance + norm_epsilon)
    normal_rows = centred * inv_scale
    return (normal_rows * gain_row + offset_row, normal_rows, inv_scale)


def norm_backward(upstream, normal_rows, inv_scale, gain_row):
    scaled = upstream * gain_row
    row_grad = inv_scale * (
        scaled
        - jnp.mean(scaled, axis=-1, keepdims=True)
        - normal_rows * jnp.mean(scaled * normal_rows, axis=-1, keepdims=True)
    )
    return (row_grad, jnp.sum(upstream * normal_rows, axis=0), jnp.sum(upstream, axis=0))


def allowed_mask(first_row, row_total, key_total, seq_length, block_size):
    row_pos = first_row + lax.broadcasted_iota(jnp.int32, (row_total, key_total), 0)
    key_pos = lax.broadcasted_iota(jnp.int32, (row_total, key_total), 1)
    return (key_pos // block_size <= row_pos // block_size) & (key_pos < seq_length)


def attend(query_rows, key_rows, value_rows, seq_length, block_size):
    row_total, local_heads, head_size = query_rows.shape
    block_rows = min(512, row_total)
    block_count = row_total // block_rows
    query_blocks = query_rows.reshape(block_count, block_rows, local_heads, head_size)

    def one_block(block_pair):
        block_index, query_block = block_pair
        scores = jnp.einsum(
            "qhd,khd->hqk", query_block, key_rows, preferred_element_type=jnp.float32
        )
        allowed = allowed_mask(
            block_index * block_rows, block_rows, row_total, seq_length, block_size
        )
        scores = jnp.where(allowed[None], scores, masked_score)
        top_score = jnp.max(scores, axis=-1, keepdims=True)
        exp_scores = jnp.exp(scores - top_score)
        exp_total = jnp.sum(exp_scores, axis=-1, keepdims=True)
        probabilities = (exp_scores / exp_total).astype(jnp.bfloat16)
        context = jnp.einsum(
            "hqk,khd->qhd", probabilities, value_rows, preferred_element_type=jnp.float32
        )
        return (context.astype(jnp.bfloat16), top_score[..., 0] + jnp.log(exp_total[..., 0]))

    contexts, log_sums = lax.map(
        one_block, (jnp.arange(block_count, dtype=jnp.int32), query_blocks)
    )
    return (contexts.reshape(row_total, local_heads * head_size), log_sums)


def attend_back(query_rows, key_rows, value_rows, context_grad, log_sums, seq_length, block_size):
    row_total, local_heads, head_size = query_rows.shape
    block_rows = min(512, row_total)
    block_count = row_total // block_rows
    query_blocks = query_rows.reshape(block_count, block_rows, local_heads, head_size)
    grad_blocks = context_grad.reshape(block_count, block_rows, local_heads, head_size)

    def one_block(running, block_pack):
        key_grad, value_grad = running
        block_index, query_block, grad_block, log_block = block_pack
        scores = jnp.einsum(
            "qhd,khd->hqk", query_block, key_rows, preferred_element_type=jnp.float32
        )
        allowed = allowed_mask(
            block_index * block_rows, block_rows, row_total, seq_length, block_size
        )
        probabilities = jnp.where(allowed[None], jnp.exp(scores - log_block[..., None]), 0.0)
        prob_grad = jnp.einsum(
            "qhd,khd->hqk", grad_block, value_rows, preferred_element_type=jnp.float32
        )
        row_dot = jnp.sum(prob_grad * probabilities, axis=-1, keepdims=True)
        score_grad = (probabilities * (prob_grad - row_dot)).astype(jnp.bfloat16)
        query_grad = jnp.einsum(
            "hqk,khd->qhd", score_grad, key_rows, preferred_element_type=jnp.float32
        )
        key_grad = key_grad + jnp.einsum(
            "hqk,qhd->khd", score_grad, query_block, preferred_element_type=jnp.float32
        )
        value_grad = value_grad + jnp.einsum(
            "hqk,qhd->khd",
            probabilities.astype(jnp.bfloat16),
            grad_block,
            preferred_element_type=jnp.float32,
        )
        return ((key_grad, value_grad), query_grad)

    empty = jnp.zeros((row_total, local_heads, head_size), jnp.float32)
    (key_grad, value_grad), query_grads = lax.scan(
        one_block,
        (empty, empty),
        (jnp.arange(block_count, dtype=jnp.int32), query_blocks, grad_blocks, log_sums),
    )
    width = local_heads * head_size
    return (
        query_grads.reshape(row_total, width),
        key_grad.reshape(row_total, width),
        value_grad.reshape(row_total, width),
    )


def on_device(
    tokens,
    seq_lens,
    block_sizes,
    w_query,
    b_query,
    w_key,
    w_value,
    b_value,
    w_out,
    b_out,
    gain_one,
    shift_one,
    w_up,
    b_up,
    w_down,
    b_down,
    gain_two,
    shift_two,
    cotangent,
):
    micro_total = seq_lens.shape[0]
    seq_rows = tokens.shape[0] // micro_total
    head_cols = w_query.shape[1]
    local_heads = head_cols // HEAD
    model_width = tokens.shape[1]
    own_cols = model_width // lax.axis_size("tensor")
    column_start = lax.axis_index("tensor") * own_cols
    query_bias = b_query.astype(jnp.float32)
    value_bias = b_value.astype(jnp.float32)
    up_bias = b_up.astype(jnp.float32)
    owned = (
        w_query,
        w_key,
        w_value,
        w_out,
        w_up,
        w_down,
        b_out,
        gain_one,
        shift_one,
        b_down,
        gain_two,
        shift_two,
    )

    def shaped(flat_rows):
        return flat_rows.reshape(seq_rows, local_heads, HEAD)

    layer_outputs = []
    input_grads = []
    totals = None
    for micro_index in range(micro_total):
        rows_in = tokens[micro_index * seq_rows : (micro_index + 1) * seq_rows]
        upstream = cotangent[micro_index * seq_rows : (micro_index + 1) * seq_rows].astype(
            jnp.float32
        )
        seq_length = seq_lens[micro_index]
        block_size = block_sizes[micro_index]
        forward_set = (
            lax.all_gather(owned[0], "dp", axis=0, tiled=True),
            lax.all_gather(owned[1], "dp", axis=0, tiled=True),
            lax.all_gather(owned[2], "dp", axis=0, tiled=True),
            lax.all_gather(owned[3], "dp", axis=1, tiled=True),
            lax.all_gather(owned[4], "dp", axis=0, tiled=True),
            lax.all_gather(owned[5], "dp", axis=1, tiled=True),
            lax.all_gather(owned[6], "dp", axis=0, tiled=True),
            lax.all_gather(owned[7], "dp", axis=0, tiled=True),
            lax.all_gather(owned[8], "dp", axis=0, tiled=True),
            lax.all_gather(owned[9], "dp", axis=0, tiled=True),
            lax.all_gather(owned[10], "dp", axis=0, tiled=True),
            lax.all_gather(owned[11], "dp", axis=0, tiled=True),
        )
        (
            full_query,
            full_key,
            full_value,
            full_out,
            full_up,
            full_down,
            full_out_bias,
            full_gain_one,
            full_shift_one,
            full_down_bias,
            full_gain_two,
            full_shift_two,
        ) = forward_set
        out_bias = full_out_bias.astype(jnp.float32)
        down_bias = full_down_bias.astype(jnp.float32)
        first_gain = full_gain_one.astype(jnp.float32)
        first_shift = full_shift_one.astype(jnp.float32)
        second_gain = full_gain_two.astype(jnp.float32)
        second_shift = full_shift_two.astype(jnp.float32)
        query_rows = ((matmul(rows_in, full_query) + query_bias) * 0.125).astype(jnp.bfloat16)
        key_rows = matmul(rows_in, full_key).astype(jnp.bfloat16)
        value_rows = (matmul(rows_in, full_value) + value_bias).astype(jnp.bfloat16)
        context, log_sums = attend(
            shaped(query_rows), shaped(key_rows), shaped(value_rows), seq_length, block_size
        )
        attended = lax.psum(matmul(context, full_out), "tensor") + out_bias
        first_norm, first_hat, first_scale = norm_forward(
            rows_in.astype(jnp.float32) + attended, first_gain, first_shift
        )
        normed = first_norm.astype(jnp.bfloat16)
        expanded = matmul(normed, full_up) + up_bias
        normal_cdf = 0.5 * (1.0 + lax.erf(expanded * inv_root_two))
        hidden = (expanded * normal_cdf).astype(jnp.bfloat16)
        lowered = lax.psum(matmul(hidden, full_down), "tensor") + down_bias
        second_norm, second_hat, second_scale = norm_forward(
            normed.astype(jnp.float32) + lowered, second_gain, second_shift
        )
        layer_outputs.append(second_norm.astype(jnp.bfloat16))
        second_grad, grad_gain_two, grad_shift_two = norm_backward(
            upstream, second_hat, second_scale, second_gain
        )
        down_bias_grad = jnp.sum(second_grad, axis=0)
        second_low = second_grad.astype(jnp.bfloat16)
        down_grad = contract_rows(hidden, second_low)
        hidden_grad = contract_cols(second_low, full_down)
        expanded_grad = hidden_grad * (
            normal_cdf + expanded * jnp.exp(-0.5 * expanded * expanded) * inv_root_tau
        )
        up_bias_grad = jnp.sum(expanded_grad, axis=0)
        expanded_low = expanded_grad.astype(jnp.bfloat16)
        up_grad = contract_rows(normed, expanded_low)
        normed_grad = lax.psum(contract_cols(expanded_low, full_up), "tensor") + second_grad
        first_grad, grad_gain_one, grad_shift_one = norm_backward(
            normed_grad, first_hat, first_scale, first_gain
        )
        out_bias_grad = jnp.sum(first_grad, axis=0)
        first_low = first_grad.astype(jnp.bfloat16)
        out_grad = contract_rows(context, first_low)
        context_grad = contract_cols(first_low, full_out).astype(jnp.bfloat16)
        query_grad, key_grad, value_grad = attend_back(
            shaped(query_rows),
            shaped(key_rows),
            shaped(value_rows),
            shaped(context_grad),
            log_sums,
            seq_length,
            block_size,
        )
        query_grad = query_grad * 0.125
        query_bias_grad = jnp.sum(query_grad, axis=0)
        value_bias_grad = jnp.sum(value_grad, axis=0)
        query_low = query_grad.astype(jnp.bfloat16)
        key_low = key_grad.astype(jnp.bfloat16)
        value_low = value_grad.astype(jnp.bfloat16)
        query_w_grad = contract_rows(rows_in, query_low)
        key_w_grad = contract_rows(rows_in, key_low)
        value_w_grad = contract_rows(rows_in, value_low)
        input_term = (
            contract_cols(query_low, full_query)
            + contract_cols(key_low, full_key)
            + contract_cols(value_low, full_value)
        )
        own_grad = lax.psum_scatter(
            input_term.astype(jnp.bfloat16), "tensor", scatter_dimension=1, tiled=True
        ).astype(jnp.float32)
        input_grads.append(
            own_grad + lax.dynamic_slice_in_dim(first_grad, column_start, own_cols, 1)
        )
        terms = (
            query_w_grad,
            query_bias_grad,
            key_w_grad,
            value_w_grad,
            value_bias_grad,
            out_grad,
            out_bias_grad,
            grad_gain_one,
            grad_shift_one,
            up_grad,
            up_bias_grad,
            down_grad,
            down_bias_grad,
            grad_gain_two,
            grad_shift_two,
        )
        if totals is None:
            totals = terms
        else:
            totals = tuple((running + addend for running, addend in zip(totals, terms)))
    summed = (
        lax.psum_scatter(totals[0], "dp", scatter_dimension=0, tiled=True),
        lax.psum_scatter(totals[2], "dp", scatter_dimension=0, tiled=True),
        lax.psum_scatter(totals[3], "dp", scatter_dimension=0, tiled=True),
        lax.psum_scatter(totals[5], "dp", scatter_dimension=1, tiled=True),
        lax.psum_scatter(totals[9], "dp", scatter_dimension=0, tiled=True),
        lax.psum_scatter(totals[11], "dp", scatter_dimension=1, tiled=True),
        lax.psum_scatter(totals[6], "dp", scatter_dimension=0, tiled=True),
        lax.psum_scatter(totals[7], "dp", scatter_dimension=0, tiled=True),
        lax.psum_scatter(totals[8], "dp", scatter_dimension=0, tiled=True),
        lax.psum_scatter(totals[12], "dp", scatter_dimension=0, tiled=True),
        lax.psum_scatter(totals[13], "dp", scatter_dimension=0, tiled=True),
        lax.psum_scatter(totals[14], "dp", scatter_dimension=0, tiled=True),
    )
    bias_sums = lax.psum((totals[1], totals[4], totals[10]), "dp")
    return (
        jnp.concatenate(layer_outputs, 0),
        jnp.concatenate(input_grads, 0),
        summed[0],
        bias_sums[0],
        summed[1],
        summed[2],
        bias_sums[1],
        summed[3],
        summed[6],
        summed[7],
        summed[8],
        summed[4],
        bias_sums[2],
        summed[5],
        summed[9],
        summed[10],
        summed[11],
    )


def solution(mesh):
    in_specs = (
        P("dp", None),
        P("dp"),
        P("dp"),
        P("dp", "tensor"),
        P("tensor"),
        P("dp", "tensor"),
        P("dp", "tensor"),
        P("tensor"),
        P("tensor", "dp"),
        P("dp"),
        P("dp"),
        P("dp"),
        P("dp", "tensor"),
        P("tensor"),
        P("tensor", "dp"),
        P("dp"),
        P("dp"),
        P("dp"),
        P("dp", None),
    )
    out_specs = (
        P("dp", None),
        P("dp", "tensor"),
        P("dp", "tensor"),
        P("tensor"),
        P("dp", "tensor"),
        P("dp", "tensor"),
        P("tensor"),
        P("tensor", "dp"),
        P("dp"),
        P("dp"),
        P("dp"),
        P("dp", "tensor"),
        P("tensor"),
        P("tensor", "dp"),
        P("dp"),
        P("dp"),
        P("dp"),
    )
    return jax.shard_map(
        on_device, mesh=mesh, in_specs=in_specs, out_specs=out_specs, check_vma=False
    )
```

profile of v0, /device:TPU:0, one launch (start us, length us, event | category | flops | bytes accessed | tf_op | source)
XLA Modules:
  0.0 1132.8 jit_solution(600460367562046693)
XLA Ops:
  8.1 33.1 %all_gather.48 = bf16[768,192]{1,0:T(8,128)(2,1)S(1)} all-gather(bf16[96,192]{1,0:T(8,128)(2,1)} %param.30), channel_id=1, replica_groups=mesh['dp'=8,'tensor'=4] {'dp'}, dimensions={0}, use_global_device_ids=true | all-gather | bytes 331776 | tf_op jit(solution)/shard_map/all_gather | solution.py:194
  41.9 2.9 fusion.122
  46.2 31.1 %all_gather.50 = bf16[768,192]{1,0:T(8,128)(2,1)S(1)} all-gather(bf16[96,192]{1,0:T(8,128)(2,1)S(1)} %copy-done.68), channel_id=1, replica_groups=mesh['dp'=8,'tensor'=4] {'dp'}, dimensions={0}, use_global_device_ids=true | all-gather | bytes 331776 | tf_op jit(solution)/shard_map/all_gather | solution.py:196
  79.4 31.1 %all_gather.49 = bf16[768,192]{1,0:T(8,128)(2,1)S(1)} all-gather(bf16[96,192]{1,0:T(8,128)(2,1)S(1)} %copy-done.69), channel_id=1, replica_groups=mesh['dp'=8,'tensor'=4] {'dp'}, dimensions={0}, use_global_device_ids=true | all-gather | bytes 331776 | tf_op jit(solution)/shard_map/all_gather | solution.py:195
  114.2 21.0 %while.66 = (s32[]{:T(128)}, bf16[2,512,3,64]{1,3,2,0:T(8,128)(2,1)S(1)}, f32[2,3,512]{2,1,0:T(4,128)S(1)}, s32[]{:T(128)}, s32[]{:T(128)}, /*index=5*/s32[2]{0:...) while((s32[]{:T(128)}, ...), condition=%wide.region_3.4_spmd, body=%wide.region_0.3_spmd.sunk | while | flops 419015680 | bytes 22240444 | solution.py:78
  122.6 2.1 fusion.305
  133.1 2.1 fusion.305
  135.8 31.2 %all_gather.51 = bf16[192,768]{0,1:T(8,128)(2,1)S(1)} all-gather(bf16[192,96]{0,1:T(8,128)(2,1)S(1)} %copy.74), channel_id=1, replica_groups=mesh['dp'=8,'tensor'=4] {'dp'}, dimensions={1}, use_global_device_ids=true | all-gather | bytes 331776 | tf_op jit(solution)/shard_map/all_gather | solution.py:197
  168.0 21.0 %while.67 = (s32[]{:T(128)}, bf16[2,512,3,64]{1,3,2,0:T(8,128)(2,1)S(1)}, f32[2,3,512]{2,1,0:T(4,128)S(1)}, s32[]{:T(128)}, s32[]{:T(128)}, /*index=5*/s32[2]{0:...) while((s32[]{:T(128)}, ...), condition=%wide.region_13.14_spmd, body=%wide.region_10.13_spmd.sunk | while | flops 419015680 | bytes 22240444 | solution.py:78
  176.4 2.1 fusion.312
  186.9 2.1 fusion.312
  189.7 2.3 fusion.178
  192.0 2.3 fusion.180
  198.3 38.0 %all-reduce.16 = (bf16[768]{0:T(1024)(128)(2,1)S(1)}, bf16[768]{0:T(1024)(128)(2,1)S(1)}, bf16[768]{0:T(1024)(128)(2,1)S(1)}, bf16[768]{0:T(1024)(128)(2,1)S(1)}...) all-reduce(bf16[768]{0:T(1024)(128)(2,1)S(1)} %dynamic-update-slice, ...), channel_id=1, replica_groups=mesh['dp'=8,'tensor'=4] {'dp'}, use_global_device_ids=true, to_apply=%add | all-reduce | flops 4608 | bytes 18432
  236.4 78.9 %all-reduce.25.cloned.1.call-done = (f32[1024,768]{1,0:T(8,128)}, f32[1024,768]{1,0:T(8,128)}) async-done(((f32[1024,768]{1,0:T(8,128)}, f32[1024,768]{1,0:T(8,128)}), (f32[1024,768]{1,0:T(8,128)}, f32[1024,768]{1,0:T(8,128)})) %all-reduce.25.cloned.1.call-update) | async-done | bytes 6291472 | tf_op jit(solution)/shard_map/psum | solution.py:233
  315.4 4.7 fusion.169
  322.6 2.1 add_convert_fusion.5
  324.7 3.3 fusion.181
  329.7 3.8 multiply_convert_fusion.3
  333.5 4.9 fusion.179
  338.5 3.1 fusion.182
  342.1 119.6 %all-reduce.23.cloned.1.call-done = (f32[1024,768]{1,0:T(8,128)}, f32[1024,768]{1,0:T(8,128)}) async-done(((f32[1024,768]{1,0:T(8,128)}, f32[1024,768]{1,0:T(8,128)}), (f32[1024,768]{1,0:T(8,128)}, f32[1024,768]{1,0:T(8,128)})) %all-reduce.23.cloned.1.call-update) | async-done | bytes 6291472 | tf_op jit(solution)/shard_map/psum | solution.py:241
  461.7 4.2 fusion.167
  467.9 3.6 convert_reduce_fusion
  471.5 4.6 fusion.161
  476.1 2.9 fusion.177
  480.4 2.8 fusion.176
  483.2 3.1 fusion.141
  486.3 3.1 fusion.132
  489.7 119.9 %all-reduce.21.cloned.1.call-done = (f32[1024,768]{1,0:T(8,128)}, f32[1024,768]{1,0:T(8,128)}) async-done(((f32[1024,768]{1,0:T(8,128)}, f32[1024,768]{1,0:T(8,128)}), (f32[1024,768]{1,0:T(8,128)}, f32[1024,768]{1,0:T(8,128)})) %all-reduce.21.cloned.1.call-update) | async-done | bytes 6291472 | tf_op jit(solution)/shard_map/psum | solution.py:259
  609.6 5.4 multiply_reduce_fusion.3
  617.0 3.6 fusion.166
  628.8 44.0 %while.68 = (s32[]{:T(128)}, f32[1024,3,64]{0,2,1:T(8,128)}, f32[1024,3,64]{0,2,1:T(8,128)}, f32[2,512,3,64]{1,3,2,0:T(8,128)}, bf16[2,512,3,64]{1,3,2,0:T(8,128...) while((s32[]{:T(128)}, f32[1024,3,64]{0,2,1:T(8,128)}, ...), condition=%wide.region_27.28_spmd.clone, body=%wide.region_25.27_spmd.clone.sunk | while | flops 1028402176 | bytes 118828048 | solution.py:121
  636.0 3.6 multiply_reduce_fusion.16
  641.4 2.6 fusion.326
  644.1 2.9 fusion.328
  647.0 3.4 fusion.327
  657.8 3.7 multiply_reduce_fusion.16
  663.2 3.0 fusion.326
  666.1 2.9 fusion.328
  669.1 3.7 fusion.327
  675.1 40.6 %while.69 = (s32[]{:T(128)}, f32[1024,3,64]{0,2,1:T(8,128)}, f32[1024,3,64]{0,2,1:T(8,128)}, f32[2,512,3,64]{1,3,2,0:T(8,128)}, bf16[2,512,3,64]{1,3,2,0:T(8,128...) while((s32[]{:T(128)}, f32[1024,3,64]{0,2,1:T(8,128)}, ...), condition=%wide.region_36.37_spmd.clone, body=%wide.region_34.36_spmd.clone.sunk | while | flops 1028402176 | bytes 114159056 | solution.py:121
  680.9 2.2 fusion.338
  683.1 2.4 multiply_reduce_fusion.17
  687.4 2.6 fusion.342
  691.9 3.4 fusion.343
  700.8 2.2 fusion.338
  703.0 2.4 multiply_reduce_fusion.17
  707.3 2.9 fusion.342
  712.1 3.6 fusion.343
  715.8 2.8 fusion.171
  731.2 2.3 copy.97
  736.4 2.3 copy.95
  741.6 2.2 copy.93
  743.9 4.0 fusion.143
  747.9 2.9 convolution_add_fusion
  750.9 3.5 fusion.139
  754.6 2.9 convolution_add_fusion.1
  761.0 37.7 %all-reduce.12 = (f32[192]{0:T(256)}, f32[192]{0:T(256)}, f32[768]{0:T(1024)S(1)}, f32[768]{0:T(1024)S(1)}, f32[768]{0:T(1024)S(1)}, /*index=5*/f32[768]{0:T(102...) all-reduce(f32[192]{0:T(256)S(1)} %add.515, ...), channel_id=1, replica_groups=mesh['dp'=8,'tensor'=4] {'dp'}, use_global_device_ids=true, to_apply=%region_41.42 | all-reduce | flops 5760 | bytes 46080 | tf_op jit(solution)/shard_map/psum | solution.py:331
  811.7 38.2 %reduce-scatter.33.cloned.1.call-done = f32[96,192]{1,0:T(8,128)} async-done(((f32[768,192]{1,0:T(8,128)}), f32[96,192]{1,0:T(8,128)}) %reduce-scatter.33.cloned.1.call-update) | async-done | bytes 73744
  850.0 65.4 %reduce-scatter.31.cloned.1.call-done = f32[96,192]{1,0:T(8,128)} async-done(((f32[768,192]{1,0:T(8,128)}), f32[96,192]{1,0:T(8,128)}) %reduce-scatter.31.cloned.1.call-update) | async-done | bytes 73744
  915.4 65.7 %reduce-scatter.29.cloned.1.call-done = f32[96,192]{1,0:T(8,128)} async-done(((f32[768,192]{1,0:T(8,128)}), f32[96,192]{1,0:T(8,128)}) %reduce-scatter.29.cloned.1.call-update) | async-done | bytes 73744
  981.1 72.0 %reduce-scatter.23.cloned.1.call-done = f32[768,96]{0,1:T(8,128)} async-done(((f32[768,768]{0,1:T(8,128)}), f32[768,96]{0,1:T(8,128)}) %reduce-scatter.23.cloned.1.call-update) | async-done | bytes 294928 | tf_op jit(solution)/shard_map/reduce_scatter | solution.py:323
  1053.1 72.1 %reduce-scatter.21.cloned.1.call-done = f32[96,768]{1,0:T(8,128)} async-done(((f32[768,768]{1,0:T(8,128)}), f32[96,768]{1,0:T(8,128)}) %reduce-scatter.21.cloned.1.call-update) | async-done | bytes 294928 | tf_op jit(solution)/shard_map/reduce_scatter | solution.py:322
  (481 shorter events, 131.1 us)
Async XLA Ops:
  8.0 36.7 %copy-start.23 = (bf16[2048,768]{1,0:T(8,128)(2,1)S(1)}, bf16[2048,768]{1,0:T(8,128)(2,1)}, u32[]{:S(2)}) copy-start(bf16[2048,768]{1,0:T(8,128)(2,1)} %param.27) | copy-start | bytes 9437188
  8.0 307.3 %all-reduce.25.cloned.1.call-start = ((), (), s32[]{:S(2)}) async-start(), calls=%async_computation.20 | async-start | bytes 12582912 | tf_op jit(solution)/shard_map/psum | solution.py:233
  41.2 5.0 copy-start.53
  41.2 5.0 copy-start.68
  41.9 35.4 %copy-start.93 = (bf16[192]{0:T(256)(128)(2,1)S(1)}, bf16[192]{0:T(256)(128)(2,1)}, u32[]{:S(2)}) copy-start(bf16[192]{0:T(256)(128)(2,1)} %param.34) | copy-start | bytes 1156
  46.2 33.2 %copy-start.69 = (bf16[96,192]{1,0:T(8,128)(2,1)S(1)}, bf16[96,192]{1,0:T(8,128)(2,1)}, u32[]{:S(2)}) copy-start(bf16[96,192]{1,0:T(8,128)(2,1)} %param.32) | copy-start | bytes 110596
  77.3 34.0 %copy-start.43 = (bf16[768,192]{1,0:T(8,128)(2,1)}, bf16[768,192]{1,0:T(8,128)(2,1)S(1)}, u32[]{:S(2)}) copy-start(bf16[768,192]{1,0:T(8,128)(2,1)S(1)} %all_gather.50) | copy-start | bytes 884740
  77.3 33.2 %copy-start.24 = (bf16[2048,768]{1,0:T(8,128)(2,1)S(1)}, bf16[2048,768]{1,0:T(8,128)(2,1)}, u32[]{:S(2)}) copy-start(bf16[2048,768]{1,0:T(8,128)(2,1)} %param.27) | copy-start | bytes 9437188
  79.4 32.5 %copy-start.64 = (bf16[1024,192]{0,1:T(8,128)(2,1)S(1)}, bf16[1024,192]{0,1:T(8,128)(2,1)}, u32[]{:S(2)}) copy-start(bf16[1024,192]{0,1:T(8,128)(2,1)} %fusion.122) | copy-start | bytes 1179652
  114.2 21.5 %copy-start.70 = (bf16[192,96]{1,0:T(8,128)(2,1)S(1)}, bf16[192,96]{1,0:T(8,128)(2,1)}, u32[]{:S(2)}) copy-start(bf16[192,96]{1,0:T(8,128)(2,1)} %param.35) | copy-start | bytes 110596
  114.2 52.8 %copy-start.63 = (bf16[1024,192]{0,1:T(8,128)(2,1)S(1)}, bf16[1024,192]{0,1:T(8,128)(2,1)}, u32[]{:S(2)}) copy-start(bf16[1024,192]{0,1:T(8,128)(2,1)} %fusion.123) | copy-start | bytes 1179652
  135.7 54.0 %copy-start.57 = (bf16[24,8,2,512]{3,1,2,0:T(8,128)(2,1)}, bf16[24,8,2,512]{3,1,2,0:T(8,128)(2,1)S(1)}, u32[]{:S(2)}) copy-start(bf16[24,8,2,512]{3,1,2,0:T(8,128)(2,1)S(1)} %copy.101) | copy-start | bytes 1179652
  189.0 5.2 copy-start.8
  189.1 5.2 copy-start.20
  189.1 5.2 copy-start.35
  189.7 4.6 copy-start.47
  194.4 42.0 %copy-start.85 = (bf16[768]{0:T(1024)(128)(2,1)S(1)}, bf16[768]{0:T(1024)(128)(2,1)}, u32[]{:S(2)}) copy-start(bf16[768]{0:T(1024)(128)(2,1)} %param.40) | copy-start | bytes 4612
  194.4 130.3 %all-gather.3.cloned.1.call-start = ((), (), s32[]{:S(2)}) async-start(), calls=%async_computation.8 | async-start | bytes 1327104 | tf_op jit(solution)/shard_map/all_gather | solution.py:198
  195.0 138.5 %all-gather.5.cloned.1.call-start = ((), (), s32[]{:S(2)}) async-start(), calls=%async_computation.9 | async-start | bytes 1327104 | tf_op jit(solution)/shard_map/all_gather | solution.py:199
  195.6 266.2 %all-reduce.23.cloned.1.call-start = ((), (), s32[]{:S(2)}) async-start(), calls=%async_computation.19 | async-start | bytes 12582912 | tf_op jit(solution)/shard_map/psum | solution.py:241
  324.7 137.1 %copy-start.40 = (bf16[1024,768]{1,0:T(8,128)(2,1)}, bf16[1024,768]{1,0:T(8,128)(2,1)S(1)}, u32[]{:S(2)}) copy-start(bf16[1024,768]{1,0:T(8,128)(2,1)S(1)} %get-tuple-element.1173) | copy-start | bytes 4718596
  324.7 5.0 copy-start.42
  324.7 5.0 copy-start.89
  333.5 5.0 copy-start.91
  333.5 5.0 copy-start.105
  341.6 268.0 %all-reduce.21.cloned.1.call-start = ((), (), s32[]{:S(2)}) async-start(), calls=%async_computation.18 | async-start | bytes 12582912 | tf_op jit(solution)/shard_map/psum | solution.py:259
  471.5 4.6 copy-start.92
  471.5 4.6 copy-start.102
  476.1 4.3 copy-start.100
  479.0 7.3 copy-start.103
  489.4 312.8 %reduce-scatter.35.cloned.1.call-start = ((), (), s32[]{:S(2)}) async-start(), calls=%async_computation.17 | async-start | bytes 884736
  609.6 5.5 copy-start.13
  609.6 5.6 copy-start.15
  609.6 6.5 copy-start.31
  609.6 7.4 copy-start.59
  627.4 176.5 %reduce-scatter.25.cloned.1.call-start = ((), (), s32[]{:S(2)}) async-start(), calls=%async_computation.12 | async-start | bytes 1966080
  628.8 46.3 %copy-start.9 = (bf16[1024,3,64]{0,2,1:T(8,128)(2,1)S(1)}, bf16[1024,3,64]{0,2,1:T(8,128)(2,1)}, u32[]{:S(2)}) copy-start(bf16[1024,3,64]{0,2,1:T(8,128)(2,1)} %copy-done.8) | copy-start | bytes 1179652
  628.8 6.5 copy-start.10
  628.8 6.5 copy-start.21
  628.8 7.2 copy-start.28
  634.2 5.5 copy-start.4
  635.3 4.4 copy-start
  641.4 5.5 copy-start.1
  650.4 6.6 copy-start.10
  650.4 6.6 copy-start.21
  650.5 7.3 copy-start.28
  656.0 5.5 copy-start.4
  657.1 4.4 copy-start
  663.2 5.9 copy-start.1
  675.3 7.7 copy-start.26
  680.8 4.6 copy-start.6
  687.4 4.5 copy-start.3
  695.3 7.7 copy-start.26
  700.7 4.6 copy-start.6
  707.3 4.8 copy-start.3
  715.8 4.6 copy-start.17
  724.0 81.1 %reduce-scatter.27.cloned.1.call-start = ((), (), s32[]{:S(2)}) async-start(), calls=%async_computation.13 | async-start | bytes 1966080
  727.8 122.2 %reduce-scatter.33.cloned.1.call-start = ((), (), s32[]{:S(2)}) async-start(), calls=%async_computation.16 | async-start | bytes 884736
  733.6 181.8 %reduce-scatter.31.cloned.1.call-start = ((), (), s32[]{:S(2)}) async-start(), calls=%async_computation.15 | async-start | bytes 884736
  738.7 242.4 %reduce-scatter.29.cloned.1.call-start = ((), (), s32[]{:S(2)}) async-start(), calls=%async_computation.14 | async-start | bytes 884736
  743.8 4.1 copy-start.32
  743.8 309.3 %reduce-scatter.23.cloned.1.call-start = ((), (), s32[]{:S(2)}) async-start(), calls=%async_computation.11 | async-start | bytes 2654208 | tf_op jit(solution)/shard_map/reduce_scatter | solution.py:323
  743.9 4.0 copy-start.106
  750.9 374.4 %reduce-scatter.21.cloned.1.call-start = ((), (), s32[]{:S(2)}) async-start(), calls=%async_computation.10 | async-start | bytes 2654208 | tf_op jit(solution)/shard_map/reduce_scatter | solution.py:322
  (75 other events, 197.2 us)
Sparse Core Ops, SparseCore 0:
  194.5 120.7 all-reduce.24
  341.7 119.9 all-reduce.22
  489.6 119.9 all-reduce.20
Sparse Core Ops, SparseCore 1:
  197.1 42.1 all-gather.2
  241.3 40.2 all-gather.4
  627.5 62.7 reduce-scatter.34
  724.1 28.2 reduce-scatter.24
  755.0 28.1 reduce-scatter.26
  787.4 62.6 reduce-scatter.32
  853.7 61.6 reduce-scatter.30
  919.5 61.5 reduce-scatter.28
  985.0 68.0 reduce-scatter.22
  1057.2 68.0 reduce-scatter.20
where the time goes:
time: 1140 us; the launch traced here: 1130 us
  waiting for transfers between devices  633 us (56%)
  blocking collectives  202 us (18%)
  matrix products  137 us (12%)
  other arithmetic  89.8 us (8%)
  local copies, waits for them, and re-layouts  43.1 us (4%)
  between operations  19.9 us (2%)
    unnamed x19, waiting for transfers between devices  171 us
    psum x1, waiting for transfers between devices, on_device(): lax.psum(contract_cols(expanded_low, full_up), 'tensor') + second_grad  120 us
    psum x1, waiting for transfers between devices, on_device(): lowered = lax.psum(matmul(hidden, full_down), 'tensor') + down_bias  120 us
    psum x1, waiting for transfers between devices, on_device(): attended = lax.psum(matmul(context, full_out), 'tensor') + out_bias  78.9 us
    reduce_scatter x1, waiting for transfers between devices, on_device(): lax.psum_scatter(totals[9], 'dp', scatter_dimension=0, tiled=True)  72.1 us
    reduce_scatter x1, waiting for transfers between devices, on_device(): lax.psum_scatter(totals[11], 'dp', scatter_dimension=1, tiled=True)  72 us
    unnamed x1, blocking collectives  38 us
    psum x1, blocking collectives, on_device(): bias_sums = lax.psum((totals[1], totals[4], totals[10]), 'dp')  37.7 us
  transfers between devices with their start and end apart: 13, of which 8 were waited for; matrix products, arithmetic and copies ran while one was open for 14% of the time, Pallas kernels for 0%

commit v1 on v0

--- a/solution.py
+++ b/solution.py
@@ -230,7 +230,7 @@
         context, log_sums = attend(
             shaped(query_rows), shaped(key_rows), shaped(value_rows), seq_length, block_size
         )
-        attended = lax.psum(matmul(context, full_out), "tensor") + out_bias
+        attended = jnp.sum(lax.all_gather(matmul(context, full_out), "tensor"), axis=0) + out_bias
         first_norm, first_hat, first_scale = norm_forward(
             rows_in.astype(jnp.float32) + attended, first_gain, first_shift
         )

time: 1140 us -> 1220 us (1.070)
  waiting for transfers between devices: 633 us -> 694 us
  other arithmetic: 89.8 us -> 110 us
    all_gather x0 -> x2, waiting for transfers between devices: none -> 84.5 us  [on_device(): lax.all_gather(matmul(context, full_out), 'tensor')]
    psum x1 -> x0, waiting for transfers between devices: 78.9 us -> none  [on_device(): attended = lax.psum(matmul(context, full_out), 'tensor') + out_bias]
    all_gather x1, waiting for transfers between devices: 0.01 us -> 33 us  [on_device(): lax.all_gather(owned[5], 'dp', axis=1, tiled=True)]
    all_gather x1, waiting for transfers between devices: 0.01 us -> 27.1 us  [on_device(): lax.all_gather(owned[4], 'dp', axis=0, tiled=True)]
    reduce_sum x0 -> x2, other arithmetic: none -> 14.9 us  [on_device(): jnp.sum(lax.all_gather(matmul(context, full_out), 'tensor'), axis=0)]
    unnamed x214 -> x222, local copies, waits for them, and re-layouts: 28.8 us -> 26.9 us
    unnamed x19 -> x20, waiting for transfers between devices: 171 us -> 171 us
  transfers between devices with their start and end apart: 13 -> 14, of which waited for: 8 -> 11; matrix products, arithmetic and copies ran while one was open for 14% -> 17% of each run, Pallas kernels for 0% -> 0%
where the time goes in v1:
time: 1220 us; the launch traced here: 1210 us
  waiting for transfers between devices  694 us (57%)
  blocking collectives  201 us (16%)
  matrix products  141 us (12%)
  other arithmetic  110 us (9%)
  local copies, waits for them, and re-layouts  41 us (3%)
  between operations  18.6 us (2%)
    unnamed x20, waiting for transfers between devices  171 us
    psum x1, waiting for transfers between devices, on_device(): lax.psum(contract_cols(expanded_low, full_up), 'tensor') + second_grad  120 us
    psum x1, waiting for transfers between devices, on_device(): lowered = lax.psum(matmul(hidden, full_down), 'tensor') + down_bias  114 us
    all_gather x2, waiting for transfers between devices, on_device(): lax.all_gather(matmul(context, full_out), 'tensor')  84.5 us
    reduce_scatter x1, waiting for transfers between devices, on_device(): lax.psum_scatter(totals[9], 'dp', scatter_dimension=0, tiled=True)  72 us
    reduce_scatter x1, waiting for transfers between devices, on_device(): lax.psum_scatter(totals[11], 'dp', scatter_dimension=1, tiled=True)  72 us
    psum x1, blocking collectives, on_device(): bias_sums = lax.psum((totals[1], totals[4], totals[10]), 'dp')  37.7 us
    unnamed x1, blocking collectives  37.5 us
  transfers between devices with their start and end apart: 14, of which 11 were waited for; matrix products, arithmetic and copies ran while one was open for 17% of the time, Pallas kernels for 0%

profile of v1, /device:TPU:0, one launch (start us, length us, event | category | flops | bytes accessed | tf_op | source)
XLA Modules:
  0.0 1213.2 jit_solution(17310380581113226937)
XLA Ops:
  7.3 33.0 %all_gather.60 = bf16[768,192]{1,0:T(8,128)(2,1)S(1)} all-gather(bf16[96,192]{1,0:T(8,128)(2,1)} %param.30), channel_id=1, replica_groups=mesh['dp'=8,'tensor'=4] {'dp'}, dimensions={0}, use_global_device_ids=true | all-gather | bytes 331776 | tf_op jit(solution)/shard_map/all_gather | solution.py:194
  43.3 31.1 %all_gather.62 = bf16[768,192]{1,0:T(8,128)(2,1)S(1)} all-gather(bf16[96,192]{1,0:T(8,128)(2,1)S(1)} %copy-done.65), channel_id=1, replica_groups=mesh['dp'=8,'tensor'=4] {'dp'}, dimensions={0}, use_global_device_ids=true | all-gather | bytes 331776 | tf_op jit(solution)/shard_map/all_gather | solution.py:196
  74.4 31.0 %all_gather.61 = bf16[768,192]{1,0:T(8,128)(2,1)S(1)} all-gather(bf16[96,192]{1,0:T(8,128)(2,1)S(1)} %copy-done.66), channel_id=1, replica_groups=mesh['dp'=8,'tensor'=4] {'dp'}, dimensions={0}, use_global_device_ids=true | all-gather | bytes 331776 | tf_op jit(solution)/shard_map/all_gather | solution.py:195
  105.4 2.2 convolution_convert_fusion.3
  111.6 21.0 %while.66 = (s32[]{:T(128)}, bf16[2,512,3,64]{1,3,2,0:T(8,128)(2,1)S(1)}, f32[2,3,512]{2,1,0:T(4,128)S(1)}, s32[]{:T(128)}, s32[]{:T(128)}, /*index=5*/s32[2]{0:...) while((s32[]{:T(128)}, ...), condition=%wide.region_3.4_spmd, body=%wide.region_0.3_spmd.sunk | while | flops 419015680 | bytes 22240444 | solution.py:78
  133.2 31.0 %all_gather.63 = bf16[192,768]{0,1:T(8,128)(2,1)S(1)} all-gather(bf16[192,96]{0,1:T(8,128)(2,1)S(1)} %copy.74), channel_id=1, replica_groups=mesh['dp'=8,'tensor'=4] {'dp'}, dimensions={1}, use_global_device_ids=true | all-gather | bytes 331776 | tf_op jit(solution)/shard_map/all_gather | solution.py:197
  164.2 2.3 fusion.178
  174.2 21.0 %while.67 = (s32[]{:T(128)}, bf16[2,512,3,64]{1,3,2,0:T(8,128)(2,1)S(1)}, f32[2,3,512]{2,1,0:T(4,128)S(1)}, s32[]{:T(128)}, s32[]{:T(128)}, /*index=5*/s32[2]{0:...) while((s32[]{:T(128)}, ...), condition=%wide.region_13.14_spmd, body=%wide.region_10.13_spmd.sunk | while | flops 419015680 | bytes 22240444 | solution.py:78
  196.4 2.3 fusion.180
  202.8 37.5 %all-reduce.15 = (bf16[768]{0:T(1024)(128)(2,1)S(1)}, bf16[768]{0:T(1024)(128)(2,1)S(1)}, bf16[768]{0:T(1024)(128)(2,1)S(1)}, bf16[768]{0:T(1024)(128)(2,1)}, bf...) all-reduce(bf16[768]{0:T(1024)(128)(2,1)S(1)} %dynamic-update-slice, ...), channel_id=1, replica_groups=mesh['dp'=8,'tensor'=4] {'dp'}, use_global_device_ids=true, to_apply=%add | all-reduce | flops 4608 | bytes 18432
  241.5 8.3 all-gather.11.cloned.1.call-done
  249.8 7.5 reduce_sum.376
  257.3 76.2 %all-gather.13.cloned.1.call-done = f32[4096,768]{1,0:T(8,128)} async-done(((f32[1024,768]{1,0:T(8,128)}), f32[4096,768]{1,0:T(8,128)}) %all-gather.13.cloned.1.call-update) | async-done | bytes 12582928 | tf_op jit(solution)/shard_map/all_gather | solution.py:233
  333.5 7.4 reduce_sum.381
  340.9 4.8 fusion.169
  347.4 2.3 add_convert_fusion.5
  349.7 27.1 %all-gather.7.cloned.1.call-done = bf16[768,768]{1,0:T(8,128)(2,1)} async-done(((bf16[96,768]{1,0:T(8,128)(2,1)}), bf16[768,768]{1,0:T(8,128)(2,1)}) %all-gather.7.cloned.1.call-update) | async-done | bytes 1179664 | tf_op jit(solution)/shard_map/all_gather | solution.py:198
  376.8 3.3 fusion.181
  381.7 3.9 multiply_convert_fusion.3
  385.6 33.0 %all-gather.9.cloned.1.call-done = bf16[768,768]{0,1:T(8,128)(2,1)} async-done(((bf16[768,96]{0,1:T(8,128)(2,1)}), bf16[768,768]{0,1:T(8,128)(2,1)}) %all-gather.9.cloned.1.call-update) | async-done | bytes 1179664 | tf_op jit(solution)/shard_map/all_gather | solution.py:199
  418.7 5.0 fusion.179
  423.7 3.1 fusion.182
  431.2 114.4 %all-reduce.21.cloned.1.call-done = (f32[1024,768]{1,0:T(8,128)}, f32[1024,768]{1,0:T(8,128)}) async-done(((f32[1024,768]{1,0:T(8,128)}, f32[1024,768]{1,0:T(8,128)}), (f32[1024,768]{1,0:T(8,128)}, f32[1024,768]{1,0:T(8,128)})) %all-reduce.21.cloned.1.call-update) | async-done | bytes 6291472 | tf_op jit(solution)/shard_map/psum | solution.py:241
  545.5 4.6 fusion.167
  552.1 3.6 convert_reduce_fusion
  555.8 4.6 fusion.161
  560.4 2.9 fusion.177
  564.6 2.9 fusion.176
  567.5 3.1 fusion.141
  570.7 3.1 fusion.132
  574.0 119.9 %all-reduce.19.cloned.1.call-done = (f32[1024,768]{1,0:T(8,128)}, f32[1024,768]{1,0:T(8,128)}) async-done(((f32[1024,768]{1,0:T(8,128)}, f32[1024,768]{1,0:T(8,128)}), (f32[1024,768]{1,0:T(8,128)}, f32[1024,768]{1,0:T(8,128)})) %all-reduce.19.cloned.1.call-update) | async-done | bytes 6291472 | tf_op jit(solution)/shard_map/psum | solution.py:259
  693.9 5.4 multiply_reduce_fusion.3
  700.4 3.6 fusion.166
  712.5 41.3 %while.68 = (s32[]{:T(128)}, f32[1024,3,64]{0,2,1:T(8,128)}, f32[1024,3,64]{0,2,1:T(8,128)}, f32[2,512,3,64]{1,3,2,0:T(8,128)}, bf16[2,512,3,64]{1,3,2,0:T(8,128...) while((s32[]{:T(128)}, f32[1024,3,64]{0,2,1:T(8,128)}, ...), condition=%wide.region_27.28_spmd.clone, body=%wide.region_25.27_spmd.clone.sunk | while | flops 1028402176 | bytes 114109880 | solution.py:121
  720.9 2.4 multiply_reduce_fusion.16
  725.0 2.7 fusion.326
  729.5 3.4 fusion.327
  738.4 2.1 fusion.322
  741.3 2.4 multiply_reduce_fusion.16
  745.4 3.0 fusion.326
  750.2 3.7 fusion.327
  756.2 40.8 %while.69 = (s32[]{:T(128)}, f32[1024,3,64]{0,2,1:T(8,128)}, f32[1024,3,64]{0,2,1:T(8,128)}, f32[2,512,3,64]{1,3,2,0:T(8,128)}, bf16[2,512,3,64]{1,3,2,0:T(8,128...) while((s32[]{:T(128)}, f32[1024,3,64]{0,2,1:T(8,128)}, ...), condition=%wide.region_36.37_spmd.clone, body=%wide.region_34.36_spmd.clone.sunk | while | flops 1028402176 | bytes 115731952 | solution.py:121
  761.9 2.3 fusion.338
  764.3 2.4 multiply_reduce_fusion.17
  768.5 2.7 fusion.342
  773.0 3.4 fusion.343
  781.9 2.3 fusion.338
  784.3 2.4 multiply_reduce_fusion.17
  788.5 3.0 fusion.342
  793.3 3.6 fusion.343
  797.0 2.9 fusion.171
  812.4 2.3 copy.97
  817.6 2.3 copy.95
  822.8 2.2 copy.93
  825.1 4.0 fusion.143
  829.1 2.9 convolution_add_fusion
  832.2 3.5 fusion.139
  835.8 2.9 convolution_add_fusion.1
  842.3 37.7 %all-reduce.12 = (f32[192]{0:T(256)}, f32[192]{0:T(256)}, f32[768]{0:T(1024)S(1)}, f32[768]{0:T(1024)S(1)}, f32[768]{0:T(1024)S(1)}, /*index=5*/f32[768]{0:T(102...) all-reduce(f32[192]{0:T(256)S(1)} %add.511, ...), channel_id=1, replica_groups=mesh['dp'=8,'tensor'=4] {'dp'}, use_global_device_ids=true, to_apply=%region_41.42 | all-reduce | flops 5760 | bytes 46080 | tf_op jit(solution)/shard_map/psum | solution.py:331
  892.9 38.2 %reduce-scatter.33.cloned.1.call-done = f32[96,192]{1,0:T(8,128)} async-done(((f32[768,192]{1,0:T(8,128)}), f32[96,192]{1,0:T(8,128)}) %reduce-scatter.33.cloned.1.call-update) | async-done | bytes 73744
  931.2 65.4 %reduce-scatter.31.cloned.1.call-done = f32[96,192]{1,0:T(8,128)} async-done(((f32[768,192]{1,0:T(8,128)}), f32[96,192]{1,0:T(8,128)}) %reduce-scatter.31.cloned.1.call-update) | async-done | bytes 73744
  996.6 65.6 %reduce-scatter.29.cloned.1.call-done = f32[96,192]{1,0:T(8,128)} async-done(((f32[768,192]{1,0:T(8,128)}), f32[96,192]{1,0:T(8,128)}) %reduce-scatter.29.cloned.1.call-update) | async-done | bytes 73744
  1062.2 72.0 %reduce-scatter.23.cloned.1.call-done = f32[768,96]{0,1:T(8,128)} async-done(((f32[768,768]{0,1:T(8,128)}), f32[768,96]{0,1:T(8,128)}) %reduce-scatter.23.cloned.1.call-update) | async-done | bytes 294928 | tf_op jit(solution)/shard_map/reduce_scatter | solution.py:323
  1134.2 72.0 %reduce-scatter.21.cloned.1.call-done = f32[96,768]{1,0:T(8,128)} async-done(((f32[768,768]{1,0:T(8,128)}), f32[96,768]{1,0:T(8,128)}) %reduce-scatter.21.cloned.1.call-update) | async-done | bytes 294928 | tf_op jit(solution)/shard_map/reduce_scatter | solution.py:322
  (486 shorter events, 152.6 us)
Async XLA Ops:
  7.2 36.1 %copy-start.65 = (bf16[96,192]{1,0:T(8,128)(2,1)S(1)}, bf16[96,192]{1,0:T(8,128)(2,1)}, u32[]{:S(2)}) copy-start(bf16[96,192]{1,0:T(8,128)(2,1)} %param.33) | copy-start | bytes 110596
  7.2 67.2 %copy-start.95 = (bf16[192]{0:T(256)(128)(2,1)S(1)}, bf16[192]{0:T(256)(128)(2,1)}, u32[]{:S(2)}) copy-start(bf16[192]{0:T(256)(128)(2,1)} %param.34) | copy-start | bytes 1156
  7.2 67.2 %copy-start.66 = (bf16[96,192]{1,0:T(8,128)(2,1)S(1)}, bf16[96,192]{1,0:T(8,128)(2,1)}, u32[]{:S(2)}) copy-start(bf16[96,192]{1,0:T(8,128)(2,1)} %param.32) | copy-start | bytes 110596
  7.2 242.6 %all-gather.11.cloned.1.call-start = ((), (), s32[]{:S(2)}) async-start(), calls=%async_computation.12 | async-start | bytes 15728640 | tf_op jit(solution)/shard_map/all_gather | solution.py:233
  40.2 126.6 %copy-start.49 = (bf16[768,192]{1,0:T(8,128)(2,1)}, bf16[768,192]{1,0:T(8,128)(2,1)S(1)}, u32[]{:S(2)}) copy-start(bf16[768,192]{1,0:T(8,128)(2,1)S(1)} %all_gather.60) | copy-start | bytes 884740
  43.0 64.6 %copy-start.89 = (s32[2]{0:T(128)S(1)}, s32[2]{0:T(128)}, u32[]{:S(2)}) copy-start(s32[2]{0:T(128)} %param.29) | copy-start | bytes 28
  43.0 65.9 %copy-start.90 = (s32[2]{0:T(128)S(1)}, s32[2]{0:T(128)}, u32[]{:S(2)}) copy-start(s32[2]{0:T(128)} %param.28) | copy-start | bytes 28
  74.4 97.6 %copy-start.39 = (bf16[768,192]{1,0:T(8,128)(2,1)}, bf16[768,192]{1,0:T(8,128)(2,1)S(1)}, u32[]{:S(2)}) copy-start(bf16[768,192]{1,0:T(8,128)(2,1)S(1)} %all_gather.62) | copy-start | bytes 884740
  105.4 64.6 %copy-start.51 = (bf16[768,192]{1,0:T(8,128)(2,1)}, bf16[768,192]{1,0:T(8,128)(2,1)S(1)}, u32[]{:S(2)}) copy-start(bf16[768,192]{1,0:T(8,128)(2,1)S(1)} %all_gather.61) | copy-start | bytes 884740
  111.6 21.5 %copy-start.67 = (bf16[192,96]{1,0:T(8,128)(2,1)S(1)}, bf16[192,96]{1,0:T(8,128)(2,1)}, u32[]{:S(2)}) copy-start(bf16[192,96]{1,0:T(8,128)(2,1)} %param.35) | copy-start | bytes 110596
  132.6 33.9 %copy-start.8 = (bf16[1024,3,64]{0,2,1:T(8,128)(2,1)}, bf16[1024,3,64]{0,2,1:T(8,128)(2,1)S(1)}, u32[]{:S(2)}) copy-start(bf16[1024,3,64]{0,2,1:T(8,128)(2,1)S(1)} %get-tuple-element.1732) | copy-start | bytes 1179652
  132.6 33.9 %copy-start.18 = (bf16[2,512,3,64]{1,3,2,0:T(8,128)(2,1)}, bf16[2,512,3,64]{1,3,2,0:T(8,128)(2,1)S(1)}, u32[]{:S(2)}) copy-start(bf16[2,512,3,64]{1,3,2,0:T(8,128)(2,1)S(1)} %get-tuple-element.1734) | copy-start | bytes 1179652
  132.6 33.9 %copy-start.32 = (bf16[1024,3,64]{0,2,1:T(8,128)(2,1)}, bf16[1024,3,64]{0,2,1:T(8,128)(2,1)S(1)}, u32[]{:S(2)}) copy-start(bf16[1024,3,64]{0,2,1:T(8,128)(2,1)S(1)} %get-tuple-element.1743) | copy-start | bytes 1179652
  132.6 33.9 %copy-start.60 = (f32[2,3,512]{2,1,0:T(4,128)}, f32[2,3,512]{2,1,0:T(4,128)S(1)}, u32[]{:S(2)}) copy-start(f32[2,3,512]{2,1,0:T(4,128)S(1)} %get-tuple-element.1674) | copy-start | bytes 36868
  133.1 33.4 %copy-start.53 = (bf16[24,8,2,512]{3,1,2,0:T(8,128)(2,1)}, bf16[24,8,2,512]{3,1,2,0:T(8,128)(2,1)S(1)}, u32[]{:S(2)}) copy-start(bf16[24,8,2,512]{3,1,2,0:T(8,128)(2,1)S(1)} %copy.101) | copy-start | bytes 1179652
  166.6 166.9 %all-gather.13.cloned.1.call-start = ((), (), s32[]{:S(2)}) async-start(), calls=%async_computation.13 | async-start | bytes 15728640 | tf_op jit(solution)/shard_map/all_gather | solution.py:233
  196.3 5.1 copy-start.96
  196.3 5.3 copy-start.97
  196.3 5.6 copy-start.98
  196.4 5.8 copy-start.99
  196.4 6.0 copy-start.100
  196.4 6.2 copy-start.101
  196.4 44.5 %copy-start.87 = (bf16[768]{0:T(1024)(128)(2,1)S(1)}, bf16[768]{0:T(1024)(128)(2,1)}, u32[]{:S(2)}) copy-start(bf16[768]{0:T(1024)(128)(2,1)} %param.40) | copy-start | bytes 4612
  198.8 178.0 %all-gather.7.cloned.1.call-start = ((), (), s32[]{:S(2)}) async-start(), calls=%async_computation.8 | async-start | bytes 1327104 | tf_op jit(solution)/shard_map/all_gather | solution.py:198
  199.5 219.2 %all-gather.9.cloned.1.call-start = ((), (), s32[]{:S(2)}) async-start(), calls=%async_computation.9 | async-start | bytes 1327104 | tf_op jit(solution)/shard_map/all_gather | solution.py:199
  200.1 345.5 %all-reduce.21.cloned.1.call-start = ((), (), s32[]{:S(2)}) async-start(), calls=%async_computation.21 | async-start | bytes 12582912 | tf_op jit(solution)/shard_map/psum | solution.py:241
  376.8 4.9 copy-start.38
  376.8 4.9 copy-start.85
  376.8 4.9 copy-start.91
  418.7 5.0 copy-start.93
  418.7 5.0 copy-start.107
  426.8 267.1 %all-reduce.19.cloned.1.call-start = ((), (), s32[]{:S(2)}) async-start(), calls=%async_computation.20 | async-start | bytes 12582912 | tf_op jit(solution)/shard_map/psum | solution.py:259
  555.7 4.6 copy-start.86
  555.7 4.6 copy-start.94
  555.7 4.6 copy-start.104
  560.3 4.3 copy-start.102
  563.3 7.4 copy-start.105
  573.8 309.7 %reduce-scatter.35.cloned.1.call-start = ((), (), s32[]{:S(2)}) async-start(), calls=%async_computation.19 | async-start | bytes 884736
  693.9 5.4 copy-start.13
  693.9 5.6 copy-start.26
  693.9 6.5 copy-start.55
  693.9 6.5 copy-start.64
  711.1 174.0 %reduce-scatter.25.cloned.1.call-start = ((), (), s32[]{:S(2)}) async-start(), calls=%async_computation.14 | async-start | bytes 1966080
  712.5 8.4 copy-start.23
  718.0 5.3 copy-start.4
  725.0 4.5 copy-start.1
  732.9 8.4 copy-start.23
  738.4 5.3 copy-start.4
  745.4 4.8 copy-start.1
  756.4 7.9 copy-start.21
  761.9 4.8 copy-start.6
  766.9 4.3 copy-start.11
  768.5 4.5 copy-start.3
  776.4 7.9 copy-start.21
  781.9 4.8 copy-start.6
  786.9 4.6 copy-start.11
  788.5 4.8 copy-start.3
  797.0 4.7 copy-start.15
  805.3 81.1 %reduce-scatter.27.cloned.1.call-start = ((), (), s32[]{:S(2)}) async-start(), calls=%async_computation.15 | async-start | bytes 1966080
  809.0 122.1 %reduce-scatter.33.cloned.1.call-start = ((), (), s32[]{:S(2)}) async-start(), calls=%async_computation.18 | async-start | bytes 884736
  814.8 181.8 %reduce-scatter.31.cloned.1.call-start = ((), (), s32[]{:S(2)}) async-start(), calls=%async_computation.17 | async-start | bytes 884736
  820.0 242.2 %reduce-scatter.29.cloned.1.call-start = ((), (), s32[]{:S(2)}) async-start(), calls=%async_computation.16 | async-start | bytes 884736
  825.1 309.1 %reduce-scatter.23.cloned.1.call-start = ((), (), s32[]{:S(2)}) async-start(), calls=%async_computation.11 | async-start | bytes 2654208 | tf_op jit(solution)/shard_map/reduce_scatter | solution.py:323
  832.1 374.1 %reduce-scatter.21.cloned.1.call-start = ((), (), s32[]{:S(2)}) async-start(), calls=%async_computation.10 | async-start | bytes 2654208 | tf_op jit(solution)/shard_map/reduce_scatter | solution.py:322
  (76 other events, 199.7 us)
Sparse Core Ops, SparseCore 0:
  166.6 83.1 all-gather.10
  251.4 82.0 all-gather.12
  335.7 41.0 all-gather.6
  378.8 39.8 all-gather.8
  426.9 118.5 all-reduce.20
  573.9 119.9 all-reduce.18
  711.3 62.7 reduce-scatter.34
  805.4 28.3 reduce-scatter.24
  836.3 28.1 reduce-scatter.26
  868.6 62.4 reduce-scatter.32
  935.0 61.5 reduce-scatter.30
  1000.7 61.4 reduce-scatter.28
  1066.3 67.8 reduce-scatter.22
  1138.1 68.0 reduce-scatter.20
